TPU v7x, 256 devices: a whole 4x4x8 slice. The times are simulated.
256 devices in a mesh: branch: 2 (over core), pair: 128 (over y, x, z).
Axes of the slice: x: 4, y: 4, z: 8, core: 2. Of those that a mesh axis runs over, the one named last changes fastest.
Arguments:
- encoder_rows: bfloat16 [256, 196, 1024], P('pair'), may hold values from -6 to 6
- pair_list: int32 [512, 2], P('pair'), may hold values from 0 to 255, as said below
- embed_weight: bfloat16 [1024, 768], P('pair'), may hold values from -0.1875 to 0.1875
- self_qkv: bfloat16 [2, 768, 2304], P('branch'), may hold values from -0.21875 to 0.21875
- self_out: bfloat16 [2, 768, 768], P('branch'), may hold values from -0.21875 to 0.21875
- cross_q: bfloat16 [2, 768, 768], P('branch'), may hold values from -0.21875 to 0.21875
- cross_kv: bfloat16 [2, 768, 1536], P('branch'), may hold values from -0.21875 to 0.21875
- cross_out: bfloat16 [2, 768, 768], P('branch'), may hold values from -0.21875 to 0.21875
Outputs:
- view_sums: float32 [2, 256, 196, 768], P('branch', 'pair')
Inputs may be any that keep to these rules, and one draw needn't show every extreme that they name: `pair_list`: pair p's first image (column 0) is one of the images p // 4 * 2 to p // 4 * 2 + 1, and every image is the first image of some pair. The second image (column 1) differs from the first and is one of the images (p // 4 - 1) * 2 to (p // 4 + 2) * 2 - 1, counted modulo 256; where p % 4 is 0 it is one of the images (p // 4 + 1) * 2 to (p // 4 + 2) * 2 - 1, and where p % 4 is 1 one of the images (p // 4 - 1) * 2 to p // 4 * 2 - 1, both modulo 256.
All inputs are finite; a program needn't handle non-finite values.
Results may differ from a plain program's by a relative error of at most 0.0034.
Values may be sent and summed in bfloat16 or wider, within the bound.
A program may use at most 64 MiB of HBM per device.

v0:
```python
import math
import jax
import jax.numpy as jnp
from jax import lax
from jax.sharding import PartitionSpec as P

HEADS = 12


def padded(x, sides, width):
    for axis, dim in sides:
        peers, length = (lax.axis_size(axis), x.shape[dim])
        up = [(i, (i + 1) % peers) for i in range(peers)]
        down = [(j, i) for i, j in up]
        last = lax.slice_in_dim(x, length - width, length, axis=dim)
        initial = lax.slice_in_dim(x, 0, width, axis=dim)
        before = lax.ppermute(last, axis, up)
        after = lax.ppermute(initial, axis, down)
        x = jnp.concatenate([before, x, after], axis=dim)
    return x


def swapped(value, axis, bit):
    mask = 2**bit
    pairs = [(source, source ^ mask) for source in range(lax.axis_size(axis))]
    return lax.ppermute(value, axis, pairs)


def layer_norm(values):
    values = values.astype(jnp.float32)
    average = jnp.mean(values, axis=-1, keepdims=True)
    centered = values - average
    spread = jnp.mean(centered * centered, axis=-1, keepdims=True)
    return (centered * lax.rsqrt(spread + 1e-06)).astype(jnp.bfloat16)


def project(values, matrix):
    leading = values.shape[:-1]
    flattened = values.reshape(-1, values.shape[-1])
    result = jnp.dot(flattened, matrix, preferred_element_type=jnp.float32)
    return result.reshape(leading + (matrix.shape[-1],))


def attend(queries, keys_in, values_in):
    pair_count, length, model_width = queries.shape
    head_dim = model_width // HEADS
    query_heads = queries.reshape(pair_count, length, HEADS, head_dim)
    key_heads = keys_in.reshape(pair_count, length, HEADS, head_dim)
    value_heads = values_in.reshape(pair_count, length, HEADS, head_dim)
    scores = jnp.einsum(
        "bqhd,bkhd->bhqk", query_heads, key_heads, preferred_element_type=jnp.float32
    ) * (1.0 / math.sqrt(head_dim))
    raised = jnp.exp(scores)
    attn_probs = (raised / jnp.sum(raised, axis=-1, keepdims=True)).astype(jnp.bfloat16)
    mixed_rows = jnp.einsum(
        "bhqk,bkhd->bqhd", attn_probs, value_heads, preferred_element_type=jnp.float32
    )
    return mixed_rows.reshape(pair_count, length, model_width).astype(jnp.bfloat16)


def attention_part(own_rows, partner_rows, w_qkv, w_self, w_query, w_pair, w_cross):
    model_width = own_rows.shape[-1]
    triple = project(layer_norm(own_rows), w_qkv).astype(jnp.bfloat16)
    attended = attend(
        triple[..., :model_width],
        triple[..., model_width : 2 * model_width],
        triple[..., 2 * model_width :],
    )
    stream = own_rows.astype(jnp.float32) + project(attended, w_self)
    query_rows = project(layer_norm(stream), w_query).astype(jnp.bfloat16)
    pair_kv = project(layer_norm(partner_rows), w_pair).astype(jnp.bfloat16)
    crossed = attend(query_rows, pair_kv[..., :model_width], pair_kv[..., model_width:])
    return stream + project(crossed, w_cross)


def select_rows(onehot, window):
    return jnp.dot(onehot.astype(jnp.bfloat16), window, preferred_element_type=jnp.float32).astype(
        jnp.bfloat16
    )


def embed_picked(onehot, window, full_embed, pair_count, tokens_per, enc_width, model_width):
    picked = select_rows(onehot, window).reshape(pair_count * tokens_per, enc_width)
    embedded_rows = jnp.dot(picked, full_embed, preferred_element_type=jnp.float32).astype(
        jnp.bfloat16
    )
    return embedded_rows.reshape(pair_count, tokens_per, model_width)


def body(encoder_rows, pair_list, embed_weight, self_qkv, self_out, cross_q, cross_kv, cross_out):
    img_local = encoder_rows.shape[0]
    tokens_per = encoder_rows.shape[1]
    enc_width = encoder_rows.shape[2]
    pair_count = pair_list.shape[0]
    views_local = self_qkv.shape[0]
    devices = lax.axis_size("pair")
    device_id = lax.axis_index("pair")
    branch_id = lax.axis_index("branch")
    image_total = img_local * devices
    window_start = (device_id - 1) * img_local
    slot_index = jnp.arange(3 * img_local, dtype=jnp.int32)
    other_onehots = []
    local_view = 0
    view_id = branch_id * views_local + local_view
    own_ids = jnp.where(view_id == 0, pair_list[:, 0], pair_list[:, 1])
    other_ids = jnp.where(view_id == 0, pair_list[:, 1], pair_list[:, 0])
    own_place = jnp.mod(own_ids - window_start, image_total)
    other_place = jnp.mod(other_ids - window_start, image_total)
    own_places = [own_place]
    own_onehots = own_place[:, None] == slot_index[None, :]
    other_onehots.append(other_place[:, None] == slot_index[None, :])
    full_embed = lax.all_gather(embed_weight, "pair", axis=0, tiled=True)
    model_width = full_embed.shape[1]
    raw_local = encoder_rows.reshape(img_local, tokens_per * enc_width)
    window = padded(raw_local, (("pair", 0),), img_local)
    own_list = [
        embed_picked(
            own_onehots, window, full_embed, pair_count, tokens_per, enc_width, model_width
        )
    ]
    partner_list = [swapped(own_list[0], "branch", 0)]
    local_view = 0
    decoded = attention_part(
        own_list[local_view],
        partner_list[local_view],
        self_qkv[local_view],
        self_out[local_view],
        cross_q[local_view],
        cross_kv[local_view],
        cross_out[local_view],
    )
    place_onehot = (slot_index[:, None] == own_places[local_view][None, :]).astype(jnp.float32)
    contribution_list = [
        jnp.dot(
            place_onehot,
            decoded.reshape(pair_count, tokens_per * model_width),
            precision=lax.Precision.HIGHEST,
        )
    ]
    contributions = jnp.stack(contribution_list, axis=0)
    rim_rows = jnp.concatenate(
        [contributions[:, :img_local], contributions[:, 2 * img_local :]], axis=1
    )
    extended = padded(rim_rows, (("pair", 1),), img_local)
    image_sums = (
        contributions[:, img_local : 2 * img_local]
        + extended[:, :img_local]
        + extended[:, 3 * img_local :]
    )
    return image_sums.reshape(views_local, img_local, tokens_per, model_width)


def solution(mesh):
    placed = (
        P("pair", None, None),
        P("pair", None),
        P("pair", None),
        P("branch", None, None),
        P("branch", None, None),
        P("branch", None, None),
        P("branch", None, None),
        P("branch", None, None),
    )
    return jax.shard_map(
        body, mesh=mesh, in_specs=placed, out_specs=P("branch", "pair", None, None), check_vma=False
    )
```

profile of v0, /device:TPU:1, one launch (start us, length us, event | category | flops | bytes accessed | tf_op | source)
XLA Modules:
  0.0 225.7 jit_solution(11989858726416793992)
XLA Ops:
  7.3 2.5 %collective-permute-start = (bf16[2,200704]{1,0:T(2,128)(2,1)}, bf16[2,200704]{1,0:T(2,128)(2,1)}, u32[]{:S(2)}, u32[]{:S(2)}) collective-permute-start(bf16[2,200704]{1,0:T(2,128)(2,1)} %bitcast.65), channel_id=1, source_target_pairs={{0,1},{1,2},{2,3},{3,4},{4,5},{5,6},{6,7},{7,8},{8,9},{9,10},{10,1... | collective-permute-start | bytes 2408456 | tf_op jit(solution)/shard_map/ppermute | solution.py:17
  9.8 8.7 %collective-permute-start.1 = (bf16[2,200704]{1,0:T(2,128)(2,1)}, bf16[2,200704]{1,0:T(2,128)(2,1)}, u32[]{:S(2)}, u32[]{:S(2)}) collective-permute-start(bf16[2,200704]{1,0:T(2,128)(2,1)} %bitcast.66), channel_id=1, source_target_pairs={{1,0},{2,1},{3,2},{4,3},{5,4},{6,5},{7,6},{8,7},{9,8},{10,9},{11,1... | collective-permute-start | bytes 2408456 | tf_op jit(solution)/shard_map/ppermute | solution.py:18
  19.2 17.0 %collective-permute-done = bf16[2,200704]{1,0:T(2,128)(2,1)} collective-permute-done((bf16[2,200704]{1,0:T(2,128)(2,1)}, bf16[2,200704]{1,0:T(2,128)(2,1)}, u32[]{:S(2)}, u32[]{:S(2)}) %collective-permute-start) | collective-permute-done | bytes 802848 | tf_op jit(solution)/shard_map/ppermute | solution.py:17
  36.3 5.6 %convolution_convert_fusion = bf16[4,200704]{1,0:T(4,128)(2,1)} fusion(bf16[2,200704]{1,0:T(2,128)(2,1)} %collective-permute-done.1, bf16[2,200704]{1,0:T(2,128)(2,1)} %bitcast.67, bf16[2,200704]{1,0:T(2,128)(2,1)} %collective-permute-done, s32[4]{0:T(128)S(1)} %fusion.31), kind=kOutput, calls=%fused_computation | convolution fusion | flops 17661976 | bytes 4014096 | tf_op jit(solution)/shard_map/dot_general | solution.py:77
  41.9 3.6 %reshape.134 = bf16[784,1024]{1,0:T(8,128)(2,1)} reshape(bf16[4,200704]{1,0:T(4,128)(2,1)} %convolution_convert_fusion) | data formatting | bytes 3211264 | tf_op jit(solution)/shard_map/reshape | solution.py:83
  45.5 68.6 %all-gather.2.cloned.1.call-done = bf16[1024,768]{1,0:T(8,128)(2,1)} async-done(((bf16[8,768]{1,0:T(8,128)(2,1)}), bf16[1024,768]{1,0:T(8,128)(2,1)}) %all-gather.2.cloned.1.call-update) | async-done | bytes 1572880 | tf_op jit(solution)/shard_map/all_gather | solution.py:112
  114.0 4.3 %convert_reduce_fusion.1 = (f32[784]{0:T(1024)S(1)}, bf16[784,768]{1,0:T(8,128)(2,1)}) fusion(bf16[784,1024]{1,0:T(8,128)(2,1)} %reshape.134, bf16[1024,768]{1,0:T(8,128)(2,1)} %all-gather.2.cloned.1.call-done), kind=kOutput, calls=%fused_computation.21 | convolution fusion | flops 1234930944 | bytes 4385856 | tf_op jit(solution)/shard_map/dot_general | solution.py:84
  118.4 2.2 reshape.135
  122.4 2.7 %fusion.17 = bf16[784,768]{1,0:T(8,128)(2,1)} fusion(bf16[784,768]{1,0:T(8,128)(2,1)} %get-tuple-element.15, f32[784]{0:T(1024)S(1)} %add_rsqrt_fusion.2, f32[784]{0:T(1024)S(1)} %broadcast_multiply_fusion.2), kind=kLoop, calls=%fused_computation.33 | loop fusion | flops 2408448 | bytes 2414720 | tf_op jit(solution)/shard_map/convert_element_type | solution.py:34
  125.1 2.2 dot_general.40
  127.3 4.8 %convolution_convert_fusion.1 = bf16[4,196,2304]{2,1,0:T(8,128)(2,1)S(1)} fusion(bf16[4,196,768]{2,1,0:T(8,128)(2,1)} %dot_general.40, bf16[1,768,2304]{2,1,0:T(8,128)(2,1)S(1)} %copy-done), kind=kOutput, calls=%fused_computation.8 | convolution fusion | flops 2776338432 | bytes 8355840 | tf_op jit(solution)/shard_map/dot_general | solution.py:40
  135.7 2.5 %copy.79 = bf16[4,196,768]{1,2,0:T(8,128)(2,1)} copy(bf16[4,196,768]{2,1,0:T(8,128)(2,1)} %get-tuple-element.9) | data formatting | bytes 2408448 | tf_op jit(solution)/shard_map/slice | solution.py:66
  138.2 2.5 %copy.77 = bf16[4,196,768]{1,2,0:T(8,128)(2,1)} copy(bf16[4,196,768]{2,1,0:T(8,128)(2,1)} %get-tuple-element.11) | data formatting | bytes 2408448 | tf_op jit(solution)/shard_map/slice | solution.py:67
  140.7 2.9 %copy.82 = bf16[4,196,768]{2,0,1:T(4,128)(2,1)} copy(bf16[4,196,768]{2,1,0:T(8,128)(2,1)} %reshape.135) | data formatting | bytes 2408448 | tf_op jit(solution)/shard_map/reshape | solution.py:87
  143.6 4.8 %collective-permute-start.2 = (bf16[4,196,768]{2,0,1:T(4,128)(2,1)}, bf16[4,196,768]{2,0,1:T(4,128)(2,1)S(1)}, u32[]{:S(2)}, u32[]{:S(2)}) collective-permute-start(bf16[4,196,768]{2,0,1:T(4,128)(2,1)} %copy.82), channel_id=1, source_target_pairs={{0,128},{128,0},{1,129},{129,1},{2,130},{130,2},{3,131},{131,3},{4... | collective-permute-start | bytes 3612680 | tf_op jit(solution)/shard_map/ppermute | solution.py:26
  150.5 2.2 fusion.20
  156.2 2.3 %convolution_convert_fusion.3 = bf16[4,196,768]{2,1,0:T(8,128)(2,1)} fusion(f32[4,196,768]{2,1,0:T(8,128)S(1)} %get-tuple-element.19, f32[4,196]{1,0:T(4,128)S(1)} %add_rsqrt_fusion.1, f32[4,196]{1,0:T(4,128)S(1)} %broadcast_multiply_fusion.1, bf16[1,768,768]{2,1,0:T(8,128)(2,1)S(1)} %copy-done.11), kind=kOutput, calls=%fused_computation.37 | convolution fusion | flops 927252480 | bytes 4798592 | tf_op jit(solution)/shard_map/dot_general | solution.py:40
  166.5 2.5 %copy.90 = bf16[4,196,768]{1,2,0:T(8,128)(2,1)} copy(bf16[4,196,768]{2,1,0:T(8,128)(2,1)} %get-tuple-element.12) | data formatting | bytes 2408448 | tf_op jit(solution)/shard_map/slice | solution.py:72
  169.0 2.5 %copy.88 = bf16[4,196,768]{1,2,0:T(8,128)(2,1)} copy(bf16[4,196,768]{2,1,0:T(8,128)(2,1)} %get-tuple-element.13) | data formatting | bytes 2408448 | tf_op jit(solution)/shard_map/slice | solution.py:72
  171.6 3.7 %fusion.1 = (f32[4,12,196]{2,1,0:T(8,128)S(1)}, f32[4,12,196,196]{2,3,1,0:T(8,128)S(1)}) fusion(bf16[4,196,12,64]{1,3,2,0:T(8,128)(2,1)S(1)} %bitcast.58, bf16[4,196,12,64]{1,3,2,0:T(8,128)(2,1)} %bitcast.61), kind=kOutput, calls=%fused_computation.7 | convolution fusion | flops 239706432 | bytes 9821952 | tf_op jit(solution)/shard_map/bqhd,bkhd->bhqk/dot_general | solution.py:50
  175.3 2.4 %fusion.19 = bf16[4,12,64,196]{3,2,1,0:T(8,128)(2,1)S(1)} fusion(bf16[4,196,12,64]{1,3,2,0:T(8,128)(2,1)S(1)} %bitcast.63, f32[4,12,196,196]{2,3,1,0:T(8,128)S(1)} %get-tuple-element.21, f32[4,12,196]{2,1,0:T(8,128)S(1)} %get-tuple-element.20), kind=kOutput, calls=%fused_computation.35 | convolution fusion | flops 242161920 | bytes 9821952 | tf_op jit(solution)/shard_map/bhqk,bkhd->bqhd/dot_general | solution.py:55
  179.8 2.4 %convolution_bitcast_fusion = f32[1,6,150528]{2,1,0:T(8,128)S(1)} fusion(f32[4,150528]{1,0:T(4,128)S(1)} %bitcast.57, s32[4]{0:T(128)S(1)} %get-tuple-element.5), kind=kOutput, calls=%fused_computation.1 | convolution fusion | flops 43352088 | bytes 6021136 | tf_op jit(solution)/shard_map/dot_general | solution.py:134
  184.4 5.8 %collective-permute-start.4 = (f32[1,2,150528]{2,1,0:T(2,128)S(1)}, f32[1,2,150528]{2,1,0:T(2,128)S(1)}, u32[]{:S(2)}, u32[]{:S(2)}) collective-permute-start(f32[1,2,150528]{2,1,0:T(2,128)S(1)} %get-tuple-element.8), channel_id=1, source_target_pairs={{1,0},{2,1},{3,2},{4,3},{5,4},{6,5},{7,6},{8,7},{9,8},{10,9},{11,1... | collective-permute-start | bytes 3612680 | tf_op jit(solution)/shard_map/ppermute | solution.py:18
  190.2 26.6 %collective-permute-done.3 = f32[1,2,150528]{2,1,0:T(2,128)S(1)} collective-permute-done((f32[1,2,150528]{2,1,0:T(2,128)S(1)}, f32[1,2,150528]{2,1,0:T(2,128)S(1)}, u32[]{:S(2)}, u32[]{:S(2)}) %collective-permute-start.3) | collective-permute-done | bytes 1204256 | tf_op jit(solution)/shard_map/ppermute | solution.py:17
  (54 shorter events, 26.7 us)
Async XLA Ops:
  6.5 120.8 %copy-start = (bf16[1,768,2304]{2,1,0:T(8,128)(2,1)S(1)}, bf16[1,768,2304]{2,1,0:T(8,128)(2,1)}, u32[]{:S(2)}) copy-start(bf16[1,768,2304]{2,1,0:T(8,128)(2,1)} %param.11) | copy-start | bytes 10616836
  6.5 107.5 %all-gather.2.cloned.1.call-start = ((), (), s32[]{:S(2)}) async-start(), calls=%async_computation | async-start | bytes 1585152 | tf_op jit(solution)/shard_map/all_gather | solution.py:112
  7.3 29.0 %collective-permute-start = (bf16[2,200704]{1,0:T(2,128)(2,1)}, bf16[2,200704]{1,0:T(2,128)(2,1)}, u32[]{:S(2)}, u32[]{:S(2)}) collective-permute-start(bf16[2,200704]{1,0:T(2,128)(2,1)} %bitcast.65), channel_id=1, source_target_pairs={{0,1},{1,2},{2,3},{3,4},{4,5},{5,6},{6,7},{7,8},{8,9},{9,10},{10,1... | collective-permute-start | bytes 2408456 | tf_op jit(solution)/shard_map/ppermute | solution.py:17
  9.8 26.5 %collective-permute-start.1 = (bf16[2,200704]{1,0:T(2,128)(2,1)}, bf16[2,200704]{1,0:T(2,128)(2,1)}, u32[]{:S(2)}, u32[]{:S(2)}) collective-permute-start(bf16[2,200704]{1,0:T(2,128)(2,1)} %bitcast.66), channel_id=1, source_target_pairs={{1,0},{2,1},{3,2},{4,3},{5,4},{6,5},{7,6},{8,7},{9,8},{10,9},{11,1... | collective-permute-start | bytes 2408456 | tf_op jit(solution)/shard_map/ppermute | solution.py:18
  140.7 7.7 %copy-start.4 = (bf16[4,196,768]{1,2,0:T(8,128)(2,1)S(1)}, bf16[4,196,768]{1,2,0:T(8,128)(2,1)}, u32[]{:S(2)}) copy-start(bf16[4,196,768]{1,2,0:T(8,128)(2,1)} %copy.79) | copy-start | bytes 3612676
  143.6 16.5 %collective-permute-start.2 = (bf16[4,196,768]{2,0,1:T(4,128)(2,1)}, bf16[4,196,768]{2,0,1:T(4,128)(2,1)S(1)}, u32[]{:S(2)}, u32[]{:S(2)}) collective-permute-start(bf16[4,196,768]{2,0,1:T(4,128)(2,1)} %copy.82), channel_id=1, source_target_pairs={{0,128},{128,0},{1,129},{129,1},{2,130},{130,2},{3,131},{131,3},{4... | collective-permute-start | bytes 3612680 | tf_op jit(solution)/shard_map/ppermute | solution.py:26
  148.4 2.1 copy-start.6
  150.5 2.2 copy-start.5
  150.5 2.2 copy-start.10
  154.1 1.4 copy-start.2
  154.1 2.1 copy-start.11
  160.7 2.1 copy-start.9
  171.6 3.7 %copy-start.7 = (bf16[4,196,768]{1,2,0:T(8,128)(2,1)S(1)}, bf16[4,196,768]{1,2,0:T(8,128)(2,1)}, u32[]{:S(2)}) copy-start(bf16[4,196,768]{1,2,0:T(8,128)(2,1)} %copy.88) | copy-start | bytes 3612676
  175.2 2.4 %copy-start.3 = (f32[4,196,768]{2,1,0:T(8,128)S(1)}, f32[4,196,768]{2,1,0:T(8,128)}, u32[]{:S(2)}) copy-start(f32[4,196,768]{2,1,0:T(8,128)} %copy-done.2) | copy-start | bytes 7225348
  175.3 2.4 %copy-start.8 = (bf16[1,768,768]{2,1,0:T(8,128)(2,1)S(1)}, bf16[1,768,768]{2,1,0:T(8,128)(2,1)}, u32[]{:S(2)}) copy-start(bf16[1,768,768]{2,1,0:T(8,128)(2,1)} %param.15) | copy-start | bytes 3538948
  183.3 33.6 %collective-permute-start.3 = (f32[1,2,150528]{2,1,0:T(2,128)S(1)}, f32[1,2,150528]{2,1,0:T(2,128)S(1)}, u32[]{:S(2)}, u32[]{:S(2)}) collective-permute-start(f32[1,2,150528]{2,1,0:T(2,128)S(1)} %get-tuple-element.7), channel_id=1, source_target_pairs={{0,1},{1,2},{2,3},{3,4},{4,5},{5,6},{6,7},{7,8},{8,9},{9,10},{10,1... | collective-permute-start | bytes 3612680 | tf_op jit(solution)/shard_map/ppermute | solution.py:17
  184.4 34.4 %copy-start.1 = (bf16[1,768,2304]{2,1,0:T(8,128)(2,1)S(1)}, bf16[1,768,2304]{2,1,0:T(8,128)(2,1)}, u32[]{:S(2)}) copy-start(bf16[1,768,2304]{2,1,0:T(8,128)(2,1)} %param.11) | copy-start | bytes 10616836
  184.4 32.4 %collective-permute-start.4 = (f32[1,2,150528]{2,1,0:T(2,128)S(1)}, f32[1,2,150528]{2,1,0:T(2,128)S(1)}, u32[]{:S(2)}, u32[]{:S(2)}) collective-permute-start(f32[1,2,150528]{2,1,0:T(2,128)S(1)} %get-tuple-element.8), channel_id=1, source_target_pairs={{1,0},{2,1},{3,2},{4,3},{5,4},{6,5},{7,6},{8,7},{9,8},{10,9},{11,1... | collective-permute-start | bytes 3612680 | tf_op jit(solution)/shard_map/ppermute | solution.py:18
Sparse Core Ops, SparseCore 0:
  10.8 103.2 all-gather.1
where the time goes:
time: 226 us
  waiting for transfers between devices  113 us (50%)
  matrix products  34.4 us (15%)
  local copies, waits for them, and re-layouts  31.5 us (14%)
  starting transfers between devices  23 us (10%)
  between operations  13.7 us (6%)
  other arithmetic  10.3 us (5%)
    all_gather x1, waiting for transfers between devices, body(): full_embed = lax.all_gather(embed_weight, 'pair', axis=0, tiled=True)  68.6 us
    ppermute x2, waiting for transfers between devices, padded(): before = lax.ppermute(last, axis, up)  43.6 us
    ppermute x2, starting transfers between devices, padded(): after = lax.ppermute(initial, axis, down)  14.5 us
    dot_general x5, matrix products, project(): result = jnp.dot(flattened, matrix, preferred_element_type=jnp.float32)  11.8 us
    dot_general x2, matrix products, attend(): jnp.einsum('bqhd,bkhd->bhqk', query_heads, key_heads, preferred_element_t...  5.76 us
    dot_general x1, matrix products, select_rows(): jnp.dot(onehot.astype(jnp.bfloat16), window, preferred_element_type=jnp.f...  5.59 us
    reshape x2, local copies, waits for them, and re-layouts, embed_picked(): return embedded_rows.reshape(pair_count, tokens_per, model_width)  5.13 us
    ppermute x1, starting transfers between devices, swapped(): return lax.ppermute(value, axis, pairs)  4.77 us
  transfers between devices with their start and end apart: 6, of which 3 were waited for; matrix products, arithmetic and copies ran while one was open for 9% of the time, Pallas kernels for 0%

commit v1 on v0

--- a/solution.py
+++ b/solution.py
@@ -109,7 +109,9 @@
     own_places = [own_place]
     own_onehots = own_place[:, None] == slot_index[None, :]
     other_onehots.append(other_place[:, None] == slot_index[None, :])
-    full_embed = lax.all_gather(embed_weight, "pair", axis=0, tiled=True)
+    full_embed = jnp.concatenate(
+        lax.all_to_all(jnp.stack([embed_weight] * lax.axis_size("pair")), "pair", 0, 0), axis=0
+    )
     model_width = full_embed.shape[1]
     raw_local = encoder_rows.reshape(img_local, tokens_per * enc_width)
     window = padded(raw_local, (("pair", 0),), img_local)

time: 226 us -> 187 us (0.83)
  waiting for transfers between devices: 113 us -> 76.2 us
  between operations: 13.7 us -> 0.29 us
  starting transfers between devices: 23 us -> 32.5 us
  local copies, waits for them, and re-layouts: 31.5 us -> 34.3 us
    all_gather x1 -> x0, waiting for transfers between devices: 68.6 us -> none  [body(): full_embed = lax.all_gather(embed_weight, 'pair', axis=0, tiled=True)]
    ppermute x2, waiting for transfers between devices: 43.6 us -> 76.2 us  [padded(): before = lax.ppermute(last, axis, up)]
    all_to_all x0 -> x1, starting transfers between devices: none -> 16.9 us  [body(): lax.all_to_all(jnp.stack([embed_weight] * lax.axis_size('pair')), 'pair',...]
    ppermute x1, starting transfers between devices: 4.77 us -> 1.55 us  [swapped(): return lax.ppermute(value, axis, pairs)]
    ppermute x2, starting transfers between devices: 3.7 us -> 0.67 us  [padded(): before = lax.ppermute(last, axis, up)]
  transfers between devices with their start and end apart: 6 -> 6, of which waited for: 3 -> 2; matrix products, arithmetic and copies ran while one was open for 9% -> 10% of each run, Pallas kernels for 0% -> 0%
where the time goes in v1:
time: 187 us; the launch traced here: 186 us
  waiting for transfers between devices  76.2 us (41%)
  matrix products  34.6 us (19%)
  local copies, waits for them, and re-layouts  34.3 us (18%)
  starting transfers between devices  32.5 us (17%)
  other arithmetic  8.38 us (4%)
    ppermute x2, waiting for transfers between devices, padded(): before = lax.ppermute(last, axis, up)  76.2 us
    all_to_all x1, starting transfers between devices, body(): lax.all_to_all(jnp.stack([embed_weight] * lax.axis_size('pair')), 'pair',...  16.9 us
    ppermute x2, starting transfers between devices, padded(): after = lax.ppermute(initial, axis, down)  13.3 us
    dot_general x5, matrix products, project(): result = jnp.dot(flattened, matrix, preferred_element_type=jnp.float32)  11.8 us
    dot_general x2, matrix products, attend(): jnp.einsum('bqhd,bkhd->bhqk', query_heads, key_heads, preferred_element_t...  5.75 us
    dot_general x1, matrix products, select_rows(): jnp.dot(onehot.astype(jnp.bfloat16), window, preferred_element_type=jnp.f...  5.58 us
    reshape x2, local copies, waits for them, and re-layouts, embed_picked(): return embedded_rows.reshape(pair_count, tokens_per, model_width)  5.15 us
    dot_general x2, matrix products, attend(): jnp.einsum('bhqk,bkhd->bqhd', attn_probs, value_heads, preferred_element_...  4.79 us
  transfers between devices with their start and end apart: 6, of which 2 were waited for; matrix products, arithmetic and copies ran while one was open for 10% of the time, Pallas kernels for 0%

profile of v1, /device:TPU:1, one launch (start us, length us, event | category | flops | bytes accessed | tf_op | source)
XLA Modules:
  0.0 186.3 jit_solution(11980038494513568980)
XLA Ops:
  0.0 2.1 %stack.4 = bf16[128,8,768]{2,1,0:T(8,128)(2,1)} broadcast(bf16[8,768]{1,0:T(8,128)(2,1)} %param.10), dimensions={1,2} | broadcast | bytes 1585152 | tf_op jit(solution)/shard_map/stack | solution.py:113
  2.1 16.9 %all-to-all-start = ((bf16[128,8,768]{2,1,0:T(8,128)(2,1)}), bf16[128,8,768]{2,1,0:T(8,128)(2,1)}, u32[]{:S(2)}, u32[]{:S(2)}) async-start(bf16[128,8,768]{2,1,0:T(8,128)(2,1)} %stack.4), calls=%async_computation | async-start | bytes 3145728 | tf_op jit(solution)/shard_map/all_to_all | solution.py:113
  19.6 6.5 %collective-permute-start.1 = (bf16[2,200704]{1,0:T(2,128)(2,1)}, bf16[2,200704]{1,0:T(2,128)(2,1)}, u32[]{:S(2)}, u32[]{:S(2)}) collective-permute-start(bf16[2,200704]{1,0:T(2,128)(2,1)} %bitcast.72), channel_id=1, source_target_pairs={{1,0},{2,1},{3,2},{4,3},{5,4},{6,5},{7,6},{8,7},{9,8},{10,9},{11,1... | collective-permute-start | bytes 2408456 | tf_op jit(solution)/shard_map/ppermute | solution.py:18
  26.1 49.7 %collective-permute-done = bf16[2,200704]{1,0:T(2,128)(2,1)} collective-permute-done((bf16[2,200704]{1,0:T(2,128)(2,1)}, bf16[2,200704]{1,0:T(2,128)(2,1)}, u32[]{:S(2)}, u32[]{:S(2)}) %collective-permute-start) | collective-permute-done | bytes 802848 | tf_op jit(solution)/shard_map/ppermute | solution.py:17
  75.8 5.6 %convolution_convert_fusion = bf16[4,200704]{1,0:T(4,128)(2,1)} fusion(bf16[2,200704]{1,0:T(2,128)(2,1)} %collective-permute-done.1, bf16[2,200704]{1,0:T(2,128)(2,1)} %bitcast.73, bf16[2,200704]{1,0:T(2,128)(2,1)} %collective-permute-done, s32[4]{0:T(128)S(1)} %fusion.36), kind=kOutput, calls=%fused_computation | convolution fusion | flops 17661976 | bytes 4014096 | tf_op jit(solution)/shard_map/dot_general | solution.py:77
  81.4 3.6 %reshape.139 = bf16[784,1024]{1,0:T(8,128)(2,1)} reshape(bf16[4,200704]{1,0:T(4,128)(2,1)} %convolution_convert_fusion) | data formatting | bytes 3211264 | tf_op jit(solution)/shard_map/reshape | solution.py:83
  85.0 4.3 %convert_reduce_fusion.1 = (f32[784]{0:T(1024)S(1)}, bf16[784,768]{1,0:T(8,128)(2,1)}) fusion(bf16[784,1024]{1,0:T(8,128)(2,1)} %reshape.139, bf16[128,8,768]{2,1,0:T(8,128)(2,1)} %all-to-all-done), kind=kOutput, calls=%fused_computation.21 | convolution fusion | flops 1234930944 | bytes 4385856 | tf_op jit(solution)/shard_map/dot_general | solution.py:84
  89.3 2.3 %reshape.141 = bf16[4,196,768]{2,1,0:T(8,128)(2,1)} reshape(bf16[784,768]{1,0:T(8,128)(2,1)} %get-tuple-element.15) | data formatting | bytes 2408448 | tf_op jit(solution)/shard_map/reshape | solution.py:87
  94.8 2.2 %dot_general.40 = bf16[4,196,768]{2,1,0:T(8,128)(2,1)} reshape(bf16[784,768]{1,0:T(8,128)(2,1)} %fusion.17) | data formatting | bytes 2408448 | tf_op jit(solution)/shard_map/dot_general | solution.py:40
  97.1 4.8 %convolution_convert_fusion.1 = bf16[4,196,2304]{2,1,0:T(8,128)(2,1)S(1)} fusion(bf16[4,196,768]{2,1,0:T(8,128)(2,1)} %dot_general.40, bf16[1,768,2304]{2,1,0:T(8,128)(2,1)S(1)} %copy-done), kind=kOutput, calls=%fused_computation.8 | convolution fusion | flops 2776338432 | bytes 8355840 | tf_op jit(solution)/shard_map/dot_general | solution.py:40
  105.4 2.5 %copy.79 = bf16[4,196,768]{1,2,0:T(8,128)(2,1)} copy(bf16[4,196,768]{2,1,0:T(8,128)(2,1)} %get-tuple-element.9) | data formatting | bytes 2408448 | tf_op jit(solution)/shard_map/slice | solution.py:66
  108.0 2.5 %copy.77 = bf16[4,196,768]{1,2,0:T(8,128)(2,1)} copy(bf16[4,196,768]{2,1,0:T(8,128)(2,1)} %get-tuple-element.11) | data formatting | bytes 2408448 | tf_op jit(solution)/shard_map/slice | solution.py:67
  110.5 2.9 %copy.82 = bf16[4,196,768]{2,0,1:T(4,128)(2,1)} copy(bf16[4,196,768]{2,1,0:T(8,128)(2,1)} %reshape.141) | data formatting | bytes 2408448 | tf_op jit(solution)/shard_map/reshape | solution.py:87
  114.9 2.1 %fusion = (f32[4,12,196]{2,1,0:T(8,128)S(1)}, f32[4,12,196,196]{2,3,1,0:T(8,128)S(1)}) fusion(bf16[4,196,12,64]{1,3,2,0:T(8,128)(2,1)S(1)} %bitcast.65, bf16[4,196,12,64]{1,3,2,0:T(8,128)(2,1)S(1)} %bitcast.66), kind=kOutput, calls=%fused_computation.6 | convolution fusion | flops 239706432 | bytes 9821952 | tf_op jit(solution)/shard_map/bqhd,bkhd->bhqk/dot_general | solution.py:50
  117.1 2.4 %fusion.20 = bf16[4,12,64,196]{3,2,1,0:T(8,128)(2,1)S(1)} fusion(bf16[4,196,12,64]{1,3,2,0:T(8,128)(2,1)S(1)} %bitcast.68, f32[4,12,196,196]{2,3,1,0:T(8,128)S(1)} %get-tuple-element.17, f32[4,12,196]{2,1,0:T(8,128)S(1)} %get-tuple-element.16), kind=kOutput, calls=%fused_computation.36 | convolution fusion | flops 242161920 | bytes 9821952 | tf_op jit(solution)/shard_map/bhqk,bkhd->bqhd/dot_general | solution.py:55
  123.0 2.3 %convolution_convert_fusion.3 = bf16[4,196,768]{2,1,0:T(8,128)(2,1)} fusion(f32[4,196,768]{2,1,0:T(8,128)S(1)} %get-tuple-element.19, f32[4,196]{1,0:T(4,128)S(1)} %add_rsqrt_fusion.1, f32[4,196]{1,0:T(4,128)S(1)} %broadcast_multiply_fusion.1, bf16[1,768,768]{2,1,0:T(8,128)(2,1)S(1)} %copy-done.13), kind=kOutput, calls=%fused_computation.39 | convolution fusion | flops 927252480 | bytes 4798592 | tf_op jit(solution)/shard_map/dot_general | solution.py:40
  130.3 2.1 %convolution_convert_fusion.2 = bf16[4,196,1536]{2,1,0:T(8,128)(2,1)S(1)} fusion(bf16[1,768,1536]{2,1,0:T(8,128)(2,1)S(1)} %copy-done.11, bf16[4,196,768]{2,0,1:T(4,128)(2,1)S(1)} %fusion.15), kind=kOutput, calls=%fused_computation.12 | convolution fusion | flops 1850892288 | bytes 5971968 | tf_op jit(solution)/shard_map/dot_general | solution.py:40
  134.0 2.5 %copy.90 = bf16[4,196,768]{1,2,0:T(8,128)(2,1)} copy(bf16[4,196,768]{2,1,0:T(8,128)(2,1)} %get-tuple-element.12) | data formatting | bytes 2408448 | tf_op jit(solution)/shard_map/slice | solution.py:72
  136.5 2.5 %copy.88 = bf16[4,196,768]{1,2,0:T(8,128)(2,1)} copy(bf16[4,196,768]{2,1,0:T(8,128)(2,1)} %get-tuple-element.13) | data formatting | bytes 2408448 | tf_op jit(solution)/shard_map/slice | solution.py:72
  139.0 3.6 %fusion.1 = (f32[4,12,196]{2,1,0:T(8,128)S(1)}, f32[4,12,196,196]{2,3,1,0:T(8,128)S(1)}) fusion(bf16[4,196,12,64]{1,3,2,0:T(8,128)(2,1)S(1)} %bitcast.64, bf16[4,196,12,64]{1,3,2,0:T(8,128)(2,1)} %bitcast.67), kind=kOutput, calls=%fused_computation.7 | convolution fusion | flops 239706432 | bytes 9821952 | tf_op jit(solution)/shard_map/bqhd,bkhd->bhqk/dot_general | solution.py:50
  142.7 2.4 %fusion.19 = bf16[4,12,64,196]{3,2,1,0:T(8,128)(2,1)S(1)} fusion(bf16[4,196,12,64]{1,3,2,0:T(8,128)(2,1)S(1)} %bitcast.69, f32[4,12,196,196]{2,3,1,0:T(8,128)S(1)} %get-tuple-element.21, f32[4,12,196]{2,1,0:T(8,128)S(1)} %get-tuple-element.20), kind=kOutput, calls=%fused_computation.35 | convolution fusion | flops 242161920 | bytes 9821952 | tf_op jit(solution)/shard_map/bhqk,bkhd->bqhd/dot_general | solution.py:55
  147.3 2.4 %convolution_bitcast_fusion = f32[1,6,150528]{2,1,0:T(8,128)S(1)} fusion(f32[4,150528]{1,0:T(4,128)S(1)} %bitcast.63, s32[4]{0:T(128)S(1)} %get-tuple-element.5), kind=kOutput, calls=%fused_computation.1 | convolution fusion | flops 43352088 | bytes 6021136 | tf_op jit(solution)/shard_map/dot_general | solution.py:136
  150.8 6.9 %collective-permute-start.4 = (f32[1,2,150528]{2,1,0:T(2,128)S(1)}, f32[1,2,150528]{2,1,0:T(2,128)S(1)}, u32[]{:S(2)}, u32[]{:S(2)}) collective-permute-start(f32[1,2,150528]{2,1,0:T(2,128)S(1)} %get-tuple-element.8), channel_id=1, source_target_pairs={{1,0},{2,1},{3,2},{4,3},{5,4},{6,5},{7,6},{8,7},{9,8},{10,9},{11,1... | collective-permute-start | bytes 3612680 | tf_op jit(solution)/shard_map/ppermute | solution.py:18
  157.7 26.6 %collective-permute-done.3 = f32[1,2,150528]{2,1,0:T(2,128)S(1)} collective-permute-done((f32[1,2,150528]{2,1,0:T(2,128)S(1)}, f32[1,2,150528]{2,1,0:T(2,128)S(1)}, u32[]{:S(2)}, u32[]{:S(2)}) %collective-permute-start.3) | collective-permute-done | bytes 1204256 | tf_op jit(solution)/shard_map/ppermute | solution.py:17
  (58 shorter events, 24.3 us)
Async XLA Ops:
  0.0 97.1 %copy-start = (bf16[1,768,2304]{2,1,0:T(8,128)(2,1)S(1)}, bf16[1,768,2304]{2,1,0:T(8,128)(2,1)}, u32[]{:S(2)}) copy-start(bf16[1,768,2304]{2,1,0:T(8,128)(2,1)} %param.11) | copy-start | bytes 10616836
  2.1 24.0 %copy-start.10 = (s32[4,2]{0,1:T(2,128)S(1)}, s32[4,2]{0,1:T(2,128)}, u32[]{:S(2)}) copy-start(s32[4,2]{0,1:T(2,128)} %param.9) | copy-start | bytes 100
  2.1 82.8 %all-to-all-start = ((bf16[128,8,768]{2,1,0:T(8,128)(2,1)}), bf16[128,8,768]{2,1,0:T(8,128)(2,1)}, u32[]{:S(2)}, u32[]{:S(2)}) async-start(bf16[128,8,768]{2,1,0:T(8,128)(2,1)} %stack.4), calls=%async_computation | async-start | bytes 3145728 | tf_op jit(solution)/shard_map/all_to_all | solution.py:113
  19.1 56.7 %collective-permute-start = (bf16[2,200704]{1,0:T(2,128)(2,1)}, bf16[2,200704]{1,0:T(2,128)(2,1)}, u32[]{:S(2)}, u32[]{:S(2)}) collective-permute-start(bf16[2,200704]{1,0:T(2,128)(2,1)} %bitcast.71), channel_id=1, source_target_pairs={{0,1},{1,2},{2,3},{3,4},{4,5},{5,6},{6,7},{7,8},{8,9},{9,10},{10,1... | collective-permute-start | bytes 2408456 | tf_op jit(solution)/shard_map/ppermute | solution.py:17
  19.6 56.1 %collective-permute-start.1 = (bf16[2,200704]{1,0:T(2,128)(2,1)}, bf16[2,200704]{1,0:T(2,128)(2,1)}, u32[]{:S(2)}, u32[]{:S(2)}) collective-permute-start(bf16[2,200704]{1,0:T(2,128)(2,1)} %bitcast.72), channel_id=1, source_target_pairs={{1,0},{2,1},{3,2},{4,3},{5,4},{6,5},{7,6},{8,7},{9,8},{10,9},{11,1... | collective-permute-start | bytes 2408456 | tf_op jit(solution)/shard_map/ppermute | solution.py:18
  91.5 1.9 %copy-start.2 = (bf16[784,768]{1,0:T(8,128)(2,1)S(1)}, bf16[784,768]{1,0:T(8,128)(2,1)}, u32[]{:S(2)}) copy-start(bf16[784,768]{1,0:T(8,128)(2,1)} %get-tuple-element.15) | copy-start | bytes 3612676
  110.5 4.4 %copy-start.5 = (bf16[4,196,768]{1,2,0:T(8,128)(2,1)S(1)}, bf16[4,196,768]{1,2,0:T(8,128)(2,1)}, u32[]{:S(2)}) copy-start(bf16[4,196,768]{1,2,0:T(8,128)(2,1)} %copy.79) | copy-start | bytes 3612676
  113.4 13.5 %collective-permute-start.2 = (bf16[4,196,768]{2,0,1:T(4,128)(2,1)}, bf16[4,196,768]{2,0,1:T(4,128)(2,1)S(1)}, u32[]{:S(2)}, u32[]{:S(2)}) collective-permute-start(bf16[4,196,768]{2,0,1:T(4,128)(2,1)} %copy.82), channel_id=1, source_target_pairs={{0,128},{128,0},{1,129},{129,1},{2,130},{130,2},{3,131},{131,3},{4... | collective-permute-start | bytes 3612680 | tf_op jit(solution)/shard_map/ppermute | solution.py:26
  114.9 2.1 %copy-start.7 = (bf16[4,196,768]{1,2,0:T(8,128)(2,1)S(1)}, bf16[4,196,768]{1,2,0:T(8,128)(2,1)}, u32[]{:S(2)}) copy-start(bf16[4,196,768]{1,2,0:T(8,128)(2,1)} %copy.77) | copy-start | bytes 3612676
  117.1 2.4 %copy-start.6 = (bf16[4,196,768]{2,1,0:T(8,128)(2,1)S(1)}, bf16[4,196,768]{2,1,0:T(8,128)(2,1)}, u32[]{:S(2)}) copy-start(bf16[4,196,768]{2,1,0:T(8,128)(2,1)} %reshape.141) | copy-start | bytes 3612676
  117.1 2.4 %copy-start.12 = (bf16[1,768,768]{2,1,0:T(8,128)(2,1)S(1)}, bf16[1,768,768]{2,1,0:T(8,128)(2,1)}, u32[]{:S(2)}) copy-start(bf16[1,768,768]{2,1,0:T(8,128)(2,1)} %param.12) | copy-start | bytes 3538948
  120.8 1.4 copy-start.3
  120.8 2.1 %copy-start.13 = (bf16[1,768,768]{2,1,0:T(8,128)(2,1)S(1)}, bf16[1,768,768]{2,1,0:T(8,128)(2,1)}, u32[]{:S(2)}) copy-start(bf16[1,768,768]{2,1,0:T(8,128)(2,1)} %param.13) | copy-start | bytes 3538948
  128.6 1.7 copy-start.11
  139.0 3.7 %copy-start.8 = (bf16[4,196,768]{1,2,0:T(8,128)(2,1)S(1)}, bf16[4,196,768]{1,2,0:T(8,128)(2,1)}, u32[]{:S(2)}) copy-start(bf16[4,196,768]{1,2,0:T(8,128)(2,1)} %copy.88) | copy-start | bytes 3612676
  142.7 2.4 %copy-start.4 = (f32[4,196,768]{2,1,0:T(8,128)S(1)}, f32[4,196,768]{2,1,0:T(8,128)}, u32[]{:S(2)}) copy-start(f32[4,196,768]{2,1,0:T(8,128)} %copy-done.3) | copy-start | bytes 7225348
  142.7 2.4 %copy-start.9 = (bf16[1,768,768]{2,1,0:T(8,128)(2,1)S(1)}, bf16[1,768,768]{2,1,0:T(8,128)(2,1)}, u32[]{:S(2)}) copy-start(bf16[1,768,768]{2,1,0:T(8,128)(2,1)} %param.15) | copy-start | bytes 3538948
  150.7 33.6 %collective-permute-start.3 = (f32[1,2,150528]{2,1,0:T(2,128)S(1)}, f32[1,2,150528]{2,1,0:T(2,128)S(1)}, u32[]{:S(2)}, u32[]{:S(2)}) collective-permute-start(f32[1,2,150528]{2,1,0:T(2,128)S(1)} %get-tuple-element.7), channel_id=1, source_target_pairs={{0,1},{1,2},{2,3},{3,4},{4,5},{5,6},{6,7},{7,8},{8,9},{9,10},{10,1... | collective-permute-start | bytes 3612680 | tf_op jit(solution)/shard_map/ppermute | solution.py:17
  150.8 35.5 %copy-start.1 = (bf16[1,768,2304]{2,1,0:T(8,128)(2,1)S(1)}, bf16[1,768,2304]{2,1,0:T(8,128)(2,1)}, u32[]{:S(2)}) copy-start(bf16[1,768,2304]{2,1,0:T(8,128)(2,1)} %param.11) | copy-start | bytes 10616836
  150.8 33.5 %collective-permute-start.4 = (f32[1,2,150528]{2,1,0:T(2,128)S(1)}, f32[1,2,150528]{2,1,0:T(2,128)S(1)}, u32[]{:S(2)}, u32[]{:S(2)}) collective-permute-start(f32[1,2,150528]{2,1,0:T(2,128)S(1)} %get-tuple-element.8), channel_id=1, source_target_pairs={{1,0},{2,1},{3,2},{4,3},{5,4},{6,5},{7,6},{8,7},{9,8},{10,9},{11,1... | collective-permute-start | bytes 3612680 | tf_op jit(solution)/shard_map/ppermute | solution.py:18
